TPU v7x, 256 devices: a whole 4x4x8 slice. The times are simulated.
256 devices in a mesh: grid: 32 (over y_lo, z, core), orb: 8 (over y_hi, x).
Axes of the slice: x: 4, y: 4 (y_hi: 2, y_lo: 2; y = y_hi * 2 + y_lo), z: 8, core: 2. Of those that a mesh axis runs over, the one named last changes fastest.
Arguments:
- orbitals: bfloat16 [64, 1769472], P('orb', 'grid'), may hold values from -6 to 6
- potential: float32 [1769472], P('grid'), may hold values from -2 to 0
- projector_atom: int32 [49152], P('grid'), may hold values from 0 to 127, as said below
- projector_cell: int32 [49152], P('grid'), may hold values from 0 to 55295
- projector_value: float32 [49152], P('grid'), may hold values from -1.5 to 1.5
- atom_strength: float32 [128], replicated, may hold values from 0.25 to 2
- ritz_rotation: bfloat16 [4, 8, 128], P(None, None, 'orb'), may hold values from -1 to 1
- panel_owner: int32 [4], replicated, may hold values from 0 to 7
Outputs:
- filtered: bfloat16 [64, 1769472], P('orb', 'grid')
- rotated: bfloat16 [128, 1769472], P('orb', 'grid')
Inputs may be any that keep to these rules, and one draw needn't show every extreme that they name: `projector_atom`: the entries e of slab s (e // 1536 = s) name atoms of slabs s - 1, s and s + 1 only, slab t holding atoms t * 4 to (t + 1) * 4 - 1.
All inputs are finite; a program needn't handle non-finite values.
Results may differ from a plain program's by a relative error of at most 0.0049.
Values may be sent and summed in bfloat16 or wider, within the bound.
A program may use at most 128 MiB of HBM per device.

v0:
```python
import jax
import jax.numpy as jnp
from jax import lax
from jax.sharding import PartitionSpec as P

NX = 96
NY = 96
REACH = 6
ATOM_DEV = 4


stencil_weights = (
    -5369.0 / 1800.0,
    12.0 / 7.0,
    -15.0 / 56.0,
    10.0 / 189.0,
    -1.0 / 112.0,
    2.0 / 1925.0,
    -1.0 / 16632.0,
)
cheb_center = 6.0
cheb_half = 6.0


def from_everyone(array, axis):
    copies = jnp.broadcast_to(array, (lax.axis_size(axis), *array.shape))
    return lax.all_to_all(copies, axis, split_axis=0, concat_axis=0, tiled=True)


def over_copies(array, axis):
    everything = from_everyone(array, axis)
    return jnp.sum(everything, axis=0)


def with_halo(block, sides, width):
    for axis, dim in sides:
        count = lax.axis_size(axis)
        forward = [(i, i + 1) for i in range(count - 1)]
        backward = [(target, source) for source, target in forward]
        low = lax.ppermute(
            lax.slice_in_dim(block, block.shape[dim] - width, None, axis=dim), axis, forward
        )
        high = lax.ppermute(lax.slice_in_dim(block, 0, width, axis=dim), axis, backward)
        block = jnp.concatenate([low, block, high], axis=dim)
    return block


def from_root(array, axis, root):
    return lax.dynamic_index_in_dim(lax.all_gather(array, axis), root, 0, keepdims=False)


def laplace(extended, cell_count, column_pos, row_pos):
    plane_cells = NX * NY
    margin = REACH * plane_cells
    middle = extended[:, margin : margin + cell_count].astype(jnp.float32)
    summed = 3.0 * stencil_weights[0] * middle
    for distance in range(1, REACH + 1):
        plane_jump = distance * plane_cells
        row_jump = distance * NX
        upper_plane = extended[:, margin + plane_jump : margin + plane_jump + cell_count].astype(
            jnp.float32
        )
        lower_plane = extended[:, margin - plane_jump : margin - plane_jump + cell_count].astype(
            jnp.float32
        )
        row_after = extended[:, margin + row_jump : margin + row_jump + cell_count].astype(
            jnp.float32
        )
        row_before = extended[:, margin - row_jump : margin - row_jump + cell_count].astype(
            jnp.float32
        )
        cell_after = extended[:, margin + distance : margin + distance + cell_count].astype(
            jnp.float32
        )
        cell_before = extended[:, margin - distance : margin - distance + cell_count].astype(
            jnp.float32
        )
        neighbours = upper_plane + lower_plane
        neighbours = (
            neighbours
            + jnp.where(row_pos + distance < NY, row_after, 0.0)
            + jnp.where(row_pos >= distance, row_before, 0.0)
        )
        neighbours = (
            neighbours
            + jnp.where(column_pos + distance < NX, cell_after, 0.0)
            + jnp.where(column_pos >= distance, cell_before, 0.0)
        )
        summed = summed + stencil_weights[distance] * neighbours
    return (middle, summed)


def combine_atoms(partial_sums, slab_index, atom_slots):
    slab_count = lax.axis_size("grid")
    atom_table = jnp.zeros((partial_sums.shape[0], (slab_count + 2) * ATOM_DEV), jnp.float32)
    atom_table = lax.dynamic_update_slice_in_dim(atom_table, partial_sums, slab_index * ATOM_DEV, 1)
    table_sums = over_copies(atom_table, "grid")
    return lax.dynamic_slice_in_dim(table_sums, slab_index * ATOM_DEV, atom_slots, 1)


def body(
    orbitals,
    potential,
    projector_atom,
    projector_cell,
    projector_value,
    atom_strength,
    ritz_rotation,
    panel_owner,
):
    panel_rows, cell_count = orbitals.shape
    margin = REACH * NX * NY
    local_cells = lax.iota(jnp.int32, cell_count)
    column_pos = local_cells % NX
    row_pos = local_cells // NX % NY
    slab_index = lax.axis_index("grid")
    atom_slots = 3 * ATOM_DEV
    relative = projector_atom - (slab_index - 1) * ATOM_DEV
    selector = (lax.iota(jnp.int32, atom_slots)[:, None] == relative[None, :]).astype(jnp.float32)
    padded_strength = jnp.pad(atom_strength, (ATOM_DEV, ATOM_DEV))
    near_strength = lax.dynamic_slice_in_dim(padded_strength, slab_index * ATOM_DEV, atom_slots)

    def hamiltonian(extended):
        middle, summed = laplace(extended, cell_count, column_pos, row_pos)
        gathered = jnp.take(middle, projector_cell, axis=1)
        weighted = gathered * projector_value
        partial_sums = lax.dot_general(
            weighted,
            selector,
            (((1,), (1,)), ((), ())),
            precision=lax.Precision.HIGHEST,
            preferred_element_type=jnp.float32,
        )
        near_sums = combine_atoms(partial_sums, slab_index, atom_slots)
        scaled = near_sums * near_strength
        spread = (
            jnp.dot(
                scaled,
                selector,
                precision=lax.Precision.HIGHEST,
                preferred_element_type=jnp.float32,
            )
            * projector_value
        )
        nonlocal_term = jnp.zeros_like(middle).at[:, projector_cell].add(spread)
        return -0.5 * summed + potential * middle + nonlocal_term

    initial = orbitals.astype(jnp.float32)
    first_extended = with_halo(orbitals, (("grid", 1),), margin)
    first_image = hamiltonian(first_extended)
    step_field = (first_image - cheb_center * initial) / cheb_half
    second_extended = with_halo(step_field, (("grid", 1),), margin)
    second = hamiltonian(second_extended)
    filtered = (2.0 * (second - cheb_center * step_field) / cheb_half - initial).astype(
        jnp.bfloat16
    )
    step_count = ritz_rotation.shape[0]
    pieces = [from_root(filtered, "orb", panel_owner[position]) for position in range(step_count)]
    stacked = jnp.concatenate(pieces, 0)
    rotation_rows = ritz_rotation.reshape(step_count * panel_rows, ritz_rotation.shape[2])
    column_total = rotation_rows.shape[1]
    block_width = max(column_total // 4, 1)
    blocks = []
    for first_column in range(0, column_total, block_width):
        part_rows = rotation_rows[:, first_column : first_column + block_width]
        product = lax.dot_general(
            part_rows, stacked, (((0,), (0,)), ((), ())), preferred_element_type=jnp.float32
        )
        blocks.append(product.astype(jnp.bfloat16))
    rotated = jnp.concatenate(blocks, 0)
    return (filtered, rotated)


def solution(mesh):
    in_specs = (
        P("orb", "grid"),
        P("grid"),
        P("grid"),
        P("grid"),
        P("grid"),
        P(),
        P(None, None, "orb"),
        P(),
    )
    out_specs = (P("orb", "grid"), P("orb", "grid"))
    return jax.shard_map(body, mesh=mesh, in_specs=in_specs, out_specs=out_specs, check_vma=False)
```

profile of v0, /device:TPU:1, one launch (start us, length us, event | category | flops | bytes accessed | tf_op | source)
XLA Modules:
  0.0 414.1 jit_solution(2198000510288957488)
XLA Ops:
  7.2 5.1 %collective-permute-start = (bf16[8,55296]{1,0:T(8,128)(2,1)}, bf16[8,55296]{1,0:T(8,128)(2,1)S(1)}, u32[]{:S(2)}, u32[]{:S(2)}) collective-permute-start(bf16[8,55296]{1,0:T(8,128)(2,1)} %param.10), channel_id=1, source_target_pairs={{8,0},{16,8},{24,16},{32,24},{40,32},{48,40},{56,48},{64,56},{72,6... | collective-permute-start | bytes 2654216 | tf_op jit(solution)/shard_map/ppermute | solution.py:43
  12.3 1.9 collective-permute-start.1
  14.2 0.7 compare_and_fusion
  15.6 11.9 %copy.295 = f32[8,55296]{0,1:T(8,128)} copy(bf16[8,55296]{1,0:T(8,128)(2,1)} %param.10) | data formatting | bytes 2654208 | tf_op jit(solution)/shard_map/convert_element_type | solution.py:55
  27.5 11.6 %gather_fusion = f32[1536,8]{1,0:T(8,128)S(1)} fusion(f32[8,55296]{0,1:T(8,128)} %copy.295, s32[2048]{0:T(1024)S(1)} %pad_clamp_fusion), kind=kCustom, calls=%fused_computation.clone | custom fusion | bytes 104448 | tf_op jit(solution)/shard_map/jit(_take)/gather | solution.py:125
  39.8 0.7 broadcast_in_dim.251
  40.6 9.1 %all-to-all-start = ((f32[32,8,136]{2,1,0:T(8,128)}), f32[32,8,136]{2,1,0:T(8,128)S(1)}, u32[]{:S(2)}, u32[]{:S(2)}) async-start(f32[32,8,136]{2,1,0:T(8,128)} %broadcast_in_dim.251), calls=%async_computation | async-start | bytes 524288 | tf_op jit(solution)/shard_map/all_to_all | solution.py:27
  49.7 0.9 broadcast_compare_fusion.4
  50.5 0.8 broadcast_compare_fusion.2
  51.4 0.8 broadcast_compare_fusion
  52.2 0.9 add_compare_fusion.4
  53.1 0.9 add_compare_fusion.2
  54.0 0.9 add_compare_fusion
  54.8 0.8 fusion.129
  55.7 0.8 fusion.127
  56.5 0.8 fusion.125
  57.3 0.8 fusion.121
  58.1 0.8 fusion.117
  58.8 0.8 fusion.113
  59.7 1.5 all-to-all-done
  61.5 1.2 copy.298
  64.9 15.0 %multiply_add_fusion = f32[8,55296]{1,0:T(8,128)S(1)} fusion(bf16[8,55296]{1,0:T(8,128)(2,1)S(1)} %copy-done.2, bf16[8,55296]{1,0:T(8,128)(2,1)S(1)} %collective-permute-done, bf16[8,55296]{1,0:T(8,128)(2,1)S(1)} %copy-done, bf16[8,110592]{1,0:T(8,128)(2,1)S(1)} %get-tuple-element.16, bf16[8,110592]{1,0:T(8,128)(2,1)S(1)} %constant_dynamic-update-slice_fusion, ...), kind=kLoop, calls=%fused_computation.185 | loop fusion | flops 47333376 | bytes 36052992 | tf_op jit(solution)/shard_map/add | solution.py:146
  79.9 14.0 %copy.297 = f32[8,55296]{0,1:T(8,128)} copy(f32[8,55296]{1,0:T(8,128)S(1)} %multiply_add_fusion) | data formatting | bytes 3538944 | tf_op jit(solution)/shard_map/add | solution.py:146
  93.9 26.6 %scatter_fusion = f32[8,55296]{0,1:T(8,128)} fusion(f32[8,55296]{0,1:T(8,128)} %copy.297, s32[1536]{0:T(1024)S(1)} %compare_select_fusion, f32[1536,8]{1,0:T(8,128)} %copy.298), kind=kCustom, calls=%fused_computation.2 | custom fusion | flops 12288 | bytes 153600 | tf_op jit(solution)/shard_map/scatter-add | solution.py:145
  120.5 15.5 %copy.299 = f32[8,55296]{1,0:T(8,128)S(1)} copy(f32[8,55296]{0,1:T(8,128)} %scatter_fusion) | data formatting | bytes 3538944 | tf_op jit(solution)/shard_map/scatter-add | solution.py:145
  136.0 1.4 fusion.105
  137.5 4.1 collective-permute-start.3
  141.6 2.2 collective-permute-start.2
  143.8 13.9 %copy.300 = f32[8,55296]{0,1:T(8,128)} copy(f32[8,55296]{1,0:T(8,128)} %fusion.105) | data formatting | bytes 3538944 | tf_op jit(solution)/shard_map/div | solution.py:151
  157.6 11.6 %gather_fusion.1 = f32[1536,8]{1,0:T(8,128)S(1)} fusion(f32[8,55296]{0,1:T(8,128)} %copy.300, s32[2048]{0:T(1024)S(1)} %pad_clamp_fusion), kind=kCustom, calls=%fused_computation.1.clone | custom fusion | bytes 104448 | tf_op jit(solution)/shard_map/jit(_take)/gather | solution.py:125
  169.3 0.9 copy.301
  170.2 1.0 fusion.132
  171.4 0.7 broadcast_in_dim.252
  172.2 7.4 %all-to-all-start.1 = ((f32[32,8,136]{2,1,0:T(8,128)}), f32[32,8,136]{2,1,0:T(8,128)S(1)}, u32[]{:S(2)}, u32[]{:S(2)}) async-start(f32[32,8,136]{2,1,0:T(8,128)} %broadcast_in_dim.252), calls=%async_computation.1 | async-start | bytes 524288 | tf_op jit(solution)/shard_map/all_to_all | solution.py:27
  179.6 1.6 broadcast_multiply_fusion
  181.3 9.9 %all-to-all-done.1 = f32[32,8,136]{2,1,0:T(8,128)S(1)} async-done(((f32[32,8,136]{2,1,0:T(8,128)}), f32[32,8,136]{2,1,0:T(8,128)S(1)}, u32[]{:S(2)}, u32[]{:S(2)}) %all-to-all-start.1) | async-done | bytes 139296 | tf_op jit(solution)/shard_map/all_to_all | solution.py:27
  191.2 1.6 fusion.5
  192.7 1.1 copy.303
  193.9 48.8 %fusion.14 = f32[8,55296]{1,0:T(8,128)} fusion(f32[8,55296]{1,0:T(8,128)} %collective-permute-done.3, f32[8,55296]{1,0:T(8,128)} %fusion.105, f32[8,55296]{1,0:T(8,128)} %collective-permute-done.2, f32[8,55296]{1,0:T(8,128)S(1)} %copy.299, bf16[8,55296]{1,0:T(8,128)(2,1)S(1)} %copy-done, f32[55296]{0:T(1024)} %broadcast_multiply_fusion, ...), kind=kLoop, calls=%fused_computation.89 | loop fusion | flops 47333376 | bytes 11280384 | tf_op jit(solution)/shard_map/add | solution.py:146
  242.7 13.9 %copy.302 = f32[8,55296]{0,1:T(8,128)} copy(f32[8,55296]{1,0:T(8,128)} %fusion.14) | data formatting | bytes 3538944 | tf_op jit(solution)/shard_map/add | solution.py:146
  256.6 26.2 %scatter_fusion.1 = f32[8,55296]{0,1:T(8,128)} fusion(f32[8,55296]{0,1:T(8,128)} %copy.302, s32[1536]{0:T(1024)S(1)} %copy-done.33, f32[1536,8]{1,0:T(8,128)S(1)} %copy.303), kind=kCustom, calls=%fused_computation.3 | custom fusion | flops 12288 | bytes 153600 | tf_op jit(solution)/shard_map/scatter-add | solution.py:145
  282.8 15.4 %copy.304 = f32[8,55296]{1,0:T(8,128)} copy(f32[8,55296]{0,1:T(8,128)} %scatter_fusion.1) | data formatting | bytes 3538944 | tf_op jit(solution)/shard_map/scatter-add | solution.py:145
  298.2 2.8 subtract_convert_fusion
  309.2 90.2 %all-gather.3.cloned.1.call-done = bf16[64,55296]{1,0:T(8,128)(2,1)} async-done(((bf16[8,55296]{1,0:T(8,128)(2,1)}), bf16[64,55296]{1,0:T(8,128)(2,1)}) %all-gather.3.cloned.1.call-update) | async-done | bytes 7077904 | tf_op jit(solution)/shard_map/all_gather | solution.py:49
  399.4 2.2 dynamic-slice_bitcast_fusion.3
  403.0 0.7 fusion.2
  403.7 0.7 fusion.1
  405.1 2.2 pad_maximum_fusion.3
  (106 shorter events, 6.8 us)
Async XLA Ops:
  7.2 56.4 %collective-permute-start = (bf16[8,55296]{1,0:T(8,128)(2,1)}, bf16[8,55296]{1,0:T(8,128)(2,1)S(1)}, u32[]{:S(2)}, u32[]{:S(2)}) collective-permute-start(bf16[8,55296]{1,0:T(8,128)(2,1)} %param.10), channel_id=1, source_target_pairs={{8,0},{16,8},{24,16},{32,24},{40,32},{48,40},{56,48},{64,56},{72,6... | collective-permute-start | bytes 2654216 | tf_op jit(solution)/shard_map/ppermute | solution.py:43
  12.3 50.4 %collective-permute-start.1 = (bf16[8,55296]{1,0:T(8,128)(2,1)}, bf16[8,55296]{1,0:T(8,128)(2,1)S(1)}, u32[]{:S(2)}, u32[]{:S(2)}) collective-permute-start(bf16[8,55296]{1,0:T(8,128)(2,1)} %param.10), channel_id=1, source_target_pairs={{0,8},{8,16},{16,24},{24,32},{32,40},{40,48},{48,56},{56,64},{64,7... | collective-permute-start | bytes 2654216 | tf_op jit(solution)/shard_map/ppermute | solution.py:40
  14.9 24.5 %copy-start.35 = (pred[1536]{0:T(1024)(128)(4,1)}, pred[1536]{0:T(1024)(128)(4,1)S(1)}, u32[]{:S(2)}) copy-start(pred[1536]{0:T(1024)(128)(4,1)S(1)} %compare_and_fusion) | copy-start | bytes 4612
  15.6 78.2 %copy-start.32 = (s32[1536]{0:T(1024)}, s32[1536]{0:T(1024)S(1)}, u32[]{:S(2)}) copy-start(s32[1536]{0:T(1024)S(1)} %compare_select_fusion) | copy-start | bytes 18436
  15.6 23.8 %copy-start.36 = (s32[1536]{0:T(1024)S(1)}, s32[1536]{0:T(1024)}, u32[]{:S(2)}) copy-start(s32[1536]{0:T(1024)} %param.12) | copy-start | bytes 18436
  15.6 23.8 %copy-start.34 = (f32[1536]{0:T(1024)S(1)}, f32[1536]{0:T(1024)}, u32[]{:S(2)}) copy-start(f32[1536]{0:T(1024)} %param.14) | copy-start | bytes 18436
  27.5 32.1 %copy-start.39 = (f32[128]{0:T(128)S(1)}, f32[128]{0:T(128)}, u32[]{:S(2)}) copy-start(f32[128]{0:T(128)} %param.15) | copy-start | bytes 1540
  39.4 23.3 %copy-start.30 = (s32[1536]{0:T(1024)}, s32[1536]{0:T(1024)S(1)}, u32[]{:S(2)}) copy-start(s32[1536]{0:T(1024)S(1)} %broadcast_subtract_fusion) | copy-start | bytes 18436
  40.6 20.7 %all-to-all-start = ((f32[32,8,136]{2,1,0:T(8,128)}), f32[32,8,136]{2,1,0:T(8,128)S(1)}, u32[]{:S(2)}, u32[]{:S(2)}) async-start(f32[32,8,136]{2,1,0:T(8,128)} %broadcast_in_dim.251), calls=%async_computation | async-start | bytes 524288 | tf_op jit(solution)/shard_map/all_to_all | solution.py:27
  55.6 7.1 %copy-start = (bf16[8,55296]{1,0:T(8,128)(2,1)S(1)}, bf16[8,55296]{1,0:T(8,128)(2,1)}, u32[]{:S(2)}) copy-start(bf16[8,55296]{1,0:T(8,128)(2,1)} %param.10) | copy-start | bytes 2654212
  59.7 3.4 copy-start.38
  62.6 0.9 copy-start.1
  62.7 1.2 copy-start.3
  62.7 1.2 copy-start.4
  62.7 1.2 copy-start.6
  62.8 1.2 copy-start.8
  62.8 1.2 copy-start.9
  62.8 1.2 copy-start.10
  62.8 1.2 copy-start.11
  62.8 1.3 copy-start.12
  62.8 1.3 copy-start.13
  62.8 1.3 copy-start.14
  62.8 1.3 copy-start.15
  62.8 1.3 copy-start.16
  62.8 1.3 copy-start.17
  62.9 1.3 copy-start.18
  62.9 1.3 copy-start.19
  62.9 1.3 copy-start.20
  62.9 1.3 copy-start.21
  62.9 1.3 copy-start.22
  62.9 1.3 copy-start.23
  62.9 1.3 copy-start.24
  62.9 1.3 copy-start.25
  62.9 1.3 copy-start.26
  62.9 1.4 copy-start.27
  63.0 1.4 copy-start.28
  63.0 1.4 copy-start.29
  63.6 1.3 copy-start.2
  137.5 56.3 %collective-permute-start.3 = (f32[8,55296]{1,0:T(8,128)}, f32[8,55296]{1,0:T(8,128)}, u32[]{:S(2)}, u32[]{:S(2)}) collective-permute-start(f32[8,55296]{1,0:T(8,128)} %fusion.105), channel_id=1, source_target_pairs={{0,8},{8,16},{16,24},{24,32},{32,40},{40,48},{48,56},{56,64},{64,7... | collective-permute-start | bytes 5308424 | tf_op jit(solution)/shard_map/ppermute | solution.py:40
  141.6 52.3 %collective-permute-start.2 = (f32[8,55296]{1,0:T(8,128)}, f32[8,55296]{1,0:T(8,128)}, u32[]{:S(2)}, u32[]{:S(2)}) collective-permute-start(f32[8,55296]{1,0:T(8,128)} %fusion.105), channel_id=1, source_target_pairs={{8,0},{16,8},{24,16},{32,24},{40,32},{48,40},{56,48},{64,56},{72,6... | collective-permute-start | bytes 5308424 | tf_op jit(solution)/shard_map/ppermute | solution.py:43
  169.3 24.5 %copy-start.5 = (pred[55296]{0:T(1024)(128)(4,1)S(1)}, pred[55296]{0:T(1024)(128)(4,1)}, u32[]{:S(2)}) copy-start(pred[55296]{0:T(1024)(128)(4,1)} %get-tuple-element.43) | copy-start | bytes 165892
  169.3 24.5 %copy-start.7 = (pred[55296]{0:T(1024)(128)(4,1)S(1)}, pred[55296]{0:T(1024)(128)(4,1)}, u32[]{:S(2)}) copy-start(pred[55296]{0:T(1024)(128)(4,1)} %get-tuple-element.44) | copy-start | bytes 165892
  172.2 19.0 %all-to-all-start.1 = ((f32[32,8,136]{2,1,0:T(8,128)}), f32[32,8,136]{2,1,0:T(8,128)S(1)}, u32[]{:S(2)}, u32[]{:S(2)}) async-start(f32[32,8,136]{2,1,0:T(8,128)} %broadcast_in_dim.252), calls=%async_computation.1 | async-start | bytes 524288 | tf_op jit(solution)/shard_map/all_to_all | solution.py:27
  179.6 219.8 %all-gather.3.cloned.1.call-start = ((), (), s32[]{:S(2)}) async-start(), calls=%async_computation.2 | async-start | bytes 7962624 | tf_op jit(solution)/shard_map/all_gather | solution.py:49
  242.7 13.9 %copy-start.33 = (s32[1536]{0:T(1024)S(1)}, s32[1536]{0:T(1024)}, u32[]{:S(2)}) copy-start(s32[1536]{0:T(1024)} %copy-done.32) | copy-start | bytes 18436
  298.2 2.8 copy-start.37
  401.6 0.7 copy-start.31
Sparse Core Ops, SparseCore 0:
  301.2 98.1 all-gather.2
where the time goes:
time: 416 us; the launch traced here: 414 us
  other arithmetic  137 us (33%)
  local copies, waits for them, and re-layouts  118 us (28%)
  waiting for transfers between devices  102 us (25%)
  starting transfers between devices  29.9 us (7%)
  between operations  22 us (5%)
  matrix products  5.62 us (1%)
    all_gather x1, waiting for transfers between devices, from_root(): lax.all_gather(array, axis)  90.2 us
    add x2, other arithmetic, hamiltonian(): return -0.5 * summed + potential * middle + nonlocal_term  63.8 us
    scatter-add x2, other arithmetic, hamiltonian(): nonlocal_term = jnp.zeros_like(middle).at[:, projector_cell].add(spread)  52.9 us
    scatter-add x2, local copies, waits for them, and re-layouts, hamiltonian(): nonlocal_term = jnp.zeros_like(middle).at[:, projector_cell].add(spread)  30.9 us
    add x2, local copies, waits for them, and re-layouts, hamiltonian(): return -0.5 * summed + potential * middle + nonlocal_term  27.9 us
    gather x4, local copies, waits for them, and re-layouts, hamiltonian(): gathered = jnp.take(middle, projector_cell, axis=1)  24.4 us
    all_to_all x2, starting transfers between devices, from_everyone(): return lax.all_to_all(copies, axis, split_axis=0, concat_axis=0, tiled=True)  16.5 us
    div x1, local copies, waits for them, and re-layouts, body(): step_field = (first_image - cheb_center * initial) / cheb_half  13.9 us
  transfers between devices with their start and end apart: 7, of which 3 were waited for; matrix products, arithmetic and copies ran while one was open for 17% of the time, Pallas kernels for 0%

commit v1 on v0

v1 whole, which is shorter than its diff:
```python
import functools

import jax
import jax.numpy as jnp
import ml_dtypes
import numpy as np
from jax import lax
from jax.experimental import pallas as pl
from jax.experimental.pallas import tpu as pltpu
from jax.sharding import PartitionSpec as P

NX = 96
NY = 96
REACH = 6
ATOM_DEV = 4
PLANE = NX * NY
DEPTH = 6
PANEL = 8
ROWS = DEPTH * PANEL
BLOCK = 256
BLOCKS = PLANE // BLOCK
PAD = 640
WINDOW = BLOCK + 2 * PAD
PHASES = 3
CHUNKS = 3
CHUNK = PLANE // CHUNKS
CHUNK_BLOCKS = CHUNK // BLOCK
ATOM_SLOTS = 16
COARSE = 512
FLOAT = jnp.float32
HALF = jnp.bfloat16
MESH = pl.DeviceIdType.MESH

stencil_weights = (
    -5369.0 / 1800.0,
    12.0 / 7.0,
    -15.0 / 56.0,
    10.0 / 189.0,
    -1.0 / 112.0,
    2.0 / 1925.0,
    -1.0 / 16632.0,
)
cheb_center = 6.0
cheb_half = 6.0
unit = stencil_weights[1]


def plane_bands():
    bands = np.zeros((PHASES, WINDOW, BLOCK), np.float32)
    for phase in range(PHASES):
        target = phase * BLOCK + np.arange(BLOCK)
        source = phase * BLOCK - PAD + np.arange(WINDOW)
        jump = source[:, None] - target[None, :]
        same_row = (source[:, None] // NX) == (target[None, :] // NX)
        for k in range(1, REACH + 1):
            weight = stencil_weights[k] / unit
            bands[phase] += weight * ((np.abs(jump) == k) & same_row)
            bands[phase] += weight * (np.abs(jump) == k * NX)
    return bands.astype(ml_dtypes.bfloat16)


def depth_band():
    band = np.zeros((DEPTH, 3 * DEPTH), np.float32)
    for z in range(DEPTH):
        for k in range(1, REACH + 1):
            band[z, DEPTH + z - k] += stencil_weights[k] / unit
            band[z, DEPTH + z + k] += stencil_weights[k] / unit
    return np.kron(band, np.eye(PANEL, dtype=np.float32))


def contract_last(left, right):
    return lax.dot_general(left, right, (((1,), (1,)), ((), ())), preferred_element_type=FLOAT)


def dot(left, right):
    return jnp.dot(left, right, preferred_element_type=FLOAT)


def filter_kernel(
    slabs,
    orbitals,
    potential,
    atom,
    cell,
    value,
    strength,
    depth_weights,
    bands_hbm,
    filtered,
    filtered_rows,
    bands,
    stack,
    padded,
    planar,
    step,
    picks,
    spots,
    table,
    sums_out,
    sums_in,
    band_sem,
    halo_send,
    halo_recv,
    sums_send,
    sums_recv,
):
    me = lax.axis_index("grid")
    after, before = lax.rem(me + 1, slabs), lax.rem(me + slabs - 1, slabs)
    after2, before2 = lax.rem(me + 2, slabs), lax.rem(me + slabs - 2, slabs)
    barrier = pltpu.get_barrier_semaphore()
    for other in (after, before, after2, before2):
        pl.semaphore_signal(barrier, inc=1, device_id={"grid": other}, device_id_type=MESH)
    band_copy = pltpu.make_async_copy(bands_hbm, bands, band_sem)
    band_copy.start()

    def halo_copies(stage, chunk):
        columns = pl.ds(chunk * CHUNK, CHUNK)
        own = stack.at[stage, pl.ds(ROWS, ROWS), columns]
        return [
            pltpu.make_async_remote_copy(
                src_ref=own,
                dst_ref=stack.at[stage, pl.ds(place, ROWS), columns],
                send_sem=halo_send.at[stage, side, chunk],
                recv_sem=halo_recv.at[stage, side, chunk],
                device_id={"grid": other},
                device_id_type=MESH,
            )
            for side, (other, place) in enumerate(((after, 0), (before, 2 * ROWS)))
        ]

    def store_own(stage, j, rows):
        stack[stage, pl.ds(ROWS, ROWS), pl.ds(pl.multiple_of(j * BLOCK, BLOCK), BLOCK)] = rows
        padded[stage, :, pl.ds(pl.multiple_of(PAD + j * BLOCK, 128), BLOCK)] = rows

    for stage in range(2):
        padded[stage, :, pl.ds(0, PAD)] = jnp.zeros((ROWS, PAD), HALF)
        padded[stage, :, pl.ds(PAD + PLANE, PAD)] = jnp.zeros((ROWS, PAD), HALF)

    for chunk in range(CHUNKS):

        def take_block(i, carry, chunk=chunk):
            j = chunk * CHUNK_BLOCKS + i
            planes = [
                orbitals[:, pl.ds(pl.multiple_of(z * PLANE + j * BLOCK, BLOCK), BLOCK)].astype(FLOAT)
                for z in range(DEPTH)
            ]
            store_own(0, j, jnp.concatenate(planes, 0).astype(HALF))
            return carry

        lax.fori_loop(0, CHUNK_BLOCKS, take_block, 0)
        if chunk == 0:
            pl.semaphore_wait(barrier, 4)
        for copy in halo_copies(0, chunk):
            copy.start()

    cells = cell[...]
    plane_of = jnp.zeros_like(cells)
    for z in range(1, DEPTH):
        plane_of = plane_of + (cells >= z * PLANE).astype(jnp.int32)
    in_plane = cells - plane_of * PLANE
    slot = atom[...] - (me - 1) * ATOM_DEV
    coarse_key = (in_plane >> 9) * (DEPTH * ATOM_SLOTS) + plane_of * ATOM_SLOTS + slot
    fine_key = in_plane & (COARSE - 1)
    entries = cells.shape[1]
    values = value[...]
    high = values.astype(HALF).astype(FLOAT)
    low = values - high

    def fill_spots(i, carry):
        row = pl.multiple_of(i * 32, 32)
        here = (lax.broadcasted_iota(jnp.int32, (32, entries), 0) + row) == fine_key
        spots[pl.ds(row, 32), :] = jnp.where(here, high, 0.0).astype(HALF)
        spots[pl.ds(row + COARSE, 32), :] = jnp.where(here, low, 0.0).astype(HALF)
        return carry

    lax.fori_loop(0, COARSE // 32, fill_spots, 0)
    table_rows = DEPTH * ATOM_SLOTS
    for start in (table_rows, 128 + table_rows):
        table[pl.ds(start, 128 - table_rows), :] = jnp.zeros((128 - table_rows, PLANE), HALF)
    groups = PLANE // COARSE
    per_round = 6
    picked = per_round * table_rows

    def fill_table(turn, carry):
        def fill_picks(i, inner):
            row = pl.multiple_of(i * 32, 32)
            here = (
                lax.broadcasted_iota(jnp.int32, (32, entries), 0) + (row + turn * picked)
            ) == coarse_key
            picks[pl.ds(row, 32), :] = jnp.where(here, 1.0, 0.0).astype(HALF)
            return inner

        lax.fori_loop(0, picked // 32, fill_picks, 0)
        full = contract_last(picks[...], spots[pl.ds(0, COARSE), :]) + contract_last(
            picks[...], spots[pl.ds(COARSE, COARSE), :]
        )
        for i in range(per_round):
            part = full[i * table_rows : (i + 1) * table_rows]
            rounded = part.astype(HALF)
            columns = pl.ds(pl.multiple_of((turn * per_round + i) * COARSE, COARSE), COARSE)
            table[pl.ds(0, table_rows), columns] = rounded
            table[pl.ds(128, table_rows), columns] = (part - rounded.astype(FLOAT)).astype(HALF)
        return carry

    lax.fori_loop(0, groups // per_round, fill_table, 0)
    band_copy.wait()

    lanes = lax.broadcasted_iota(jnp.int32, (PANEL, 128), 1)
    near_strength = pltpu.roll(
        jnp.broadcast_to(strength[...], (PANEL, 128)),
        lax.rem(128 + ATOM_DEV - me * ATOM_DEV, 128),
        1,
    )
    column_of = lax.broadcasted_iota(jnp.int32, (ROWS, 3 * ROWS), 1)
    has_before = (me > 0).astype(FLOAT)
    has_after = (me < slabs - 1).astype(FLOAT)
    keep = jnp.where(
        column_of < ROWS, has_before, jnp.where(column_of >= 2 * ROWS, has_after, 1.0)
    )
    across = (depth_weights[...] * keep).astype(HALF)
    plane_lanes = [(lanes >= z * ATOM_SLOTS) & (lanes < (z + 1) * ATOM_SLOTS) for z in range(DEPTH)]
    partners = ((after, 124), (before, 4), (after2, 120), (before2, 8))

    def send_sums(stage):
        def add_part(i, total):
            columns = pl.ds(pl.multiple_of(i * 1024, 1024), 1024)
            return total + contract_last(
                stack[stage, pl.ds(ROWS, ROWS), columns], table[:, columns]
            )

        found = lax.fori_loop(0, PLANE // 1024, add_part, jnp.zeros((ROWS, 256), FLOAT))
        both = found[:, :128] + found[:, 128:]
        own = jnp.zeros((PANEL, 128), FLOAT)
        for z in range(DEPTH):
            part = jnp.where(plane_lanes[z], both[z * PANEL : (z + 1) * PANEL], 0.0)
            own = own + (part if z == 0 else pltpu.roll(part, 128 - z * ATOM_SLOTS, 1))
        sums_out[stage] = own
        copies = [
            pltpu.make_async_remote_copy(
                src_ref=sums_out.at[stage],
                dst_ref=sums_in.at[stage, k],
                send_sem=sums_send.at[stage, k],
                recv_sem=sums_recv.at[stage, k],
                device_id={"grid": other},
                device_id_type=MESH,
            )
            for k, (other, _) in enumerate(partners)
        ]
        for copy in copies:
            copy.start()
        return copies

    def planar_part(stage):
        for phase in range(PHASES):
            windows = [
                padded[stage, :, pl.ds((i * PHASES + phase) * BLOCK, WINDOW)]
                for i in range(BLOCKS // PHASES)
            ]
            product = dot(jnp.concatenate(windows, 0), bands[phase])
            for i in range(BLOCKS // PHASES):
                planar[:, pl.ds((i * PHASES + phase) * BLOCK, BLOCK)] = product[
                    i * ROWS : (i + 1) * ROWS
                ]

    def coupling(stage, copies):
        for copy in copies:
            copy.wait()
        total = sums_out[stage]
        for k, (_, turn) in enumerate(partners):
            total = total + pltpu.roll(sums_in[stage, k], turn, 1)
        scaled = jnp.where(plane_lanes[0], total * near_strength, 0.0)
        blocks = [
            scaled if z == 0 else pltpu.roll(scaled, z * ATOM_SLOTS, 1) for z in range(DEPTH)
        ]
        spread = jnp.concatenate(blocks, 0)
        rounded = spread.astype(HALF)
        rest = (spread - rounded.astype(FLOAT)).astype(HALF)
        return jnp.concatenate([rounded, rounded], 1), rest

    def image(stage, j, main, rest, middle):
        columns = pl.ds(pl.multiple_of(j * BLOCK, BLOCK), BLOCK)
        neighbours = planar[:, columns] + dot(across, stack[stage, :, columns])
        nonlocal_part = dot(main, table[:, columns]) + dot(rest, table[pl.ds(0, 128), columns])
        rows = []
        for z in range(DEPTH):
            halves = [
                jnp.broadcast_to(
                    potential[pl.ds(z * (PLANE // 128) + j * (BLOCK // 128) + h, 1), :], (PANEL, 128)
                )
                for h in range(BLOCK // 128)
            ]
            rows.append(jnp.concatenate(halves, 1))
        local = (jnp.concatenate(rows, 0) - (1.5 * stencil_weights[0] + cheb_center)) * (
            1.0 / cheb_half
        )
        return (
            middle * local
            - (0.5 * unit / cheb_half) * neighbours
            + nonlocal_part * (1.0 / cheb_half)
        )

    sums = send_sums(0)
    planar_part(0)
    main, rest = coupling(0, sums)
    for chunk in range(CHUNKS):
        for copy in halo_copies(0, chunk):
            copy.wait()

        def first_block(i, carry, chunk=chunk):
            j = chunk * CHUNK_BLOCKS + i
            columns = pl.ds(pl.multiple_of(j * BLOCK, BLOCK), BLOCK)
            middle = stack[0, pl.ds(ROWS, ROWS), columns].astype(FLOAT)
            field = image(0, j, main, rest, middle)
            step[:, columns] = field
            store_own(1, j, field.astype(HALF))
            return carry

        lax.fori_loop(0, CHUNK_BLOCKS, first_block, 0)
        for copy in halo_copies(1, chunk):
            copy.start()

    sums = send_sums(1)
    planar_part(1)
    main, rest = coupling(1, sums)
    for chunk in range(CHUNKS):
        for copy in halo_copies(1, chunk):
            copy.wait()

        def second_block(i, carry, chunk=chunk):
            j = chunk * CHUNK_BLOCKS + i
            columns = pl.ds(pl.multiple_of(j * BLOCK, BLOCK), BLOCK)
            initial = stack[0, pl.ds(ROWS, ROWS), columns].astype(FLOAT)
            field = 2.0 * image(1, j, main, rest, step[:, columns]) - initial
            filtered_rows[:, columns] = field.astype(HALF)
            for z in range(DEPTH):
                filtered[:, pl.ds(pl.multiple_of(z * PLANE + j * BLOCK, BLOCK), BLOCK)] = field[
                    z * PANEL : (z + 1) * PANEL
                ].astype(HALF)
            return carry

        lax.fori_loop(0, CHUNK_BLOCKS, second_block, 0)


PIECES = 3


def rotate_kernel(
    panels,
    source_rows,
    own_rotation,
    spread_index,
    spread_plane,
    rotated,
    rotations,
    wide,
    gathered,
    products,
    landed,
    local_sem,
    rot_send,
    rot_recv,
    in_send,
    in_recv,
    out_send,
    out_recv,
):
    me = lax.axis_index("orb")
    width = PLANE // panels
    piece = width // PIECES
    columns_out = own_rotation.shape[0]
    barrier = pltpu.get_barrier_semaphore()
    others = [lax.rem(me + k, panels) for k in range(1, panels)]
    for other in others:
        pl.semaphore_signal(barrier, inc=1, device_id={"orb": other}, device_id_type=MESH)

    def at(index, size):
        return pl.ds(pl.multiple_of(index * size, size), size)

    def columns(owner, part):
        return pl.ds(pl.multiple_of(owner * width + part * piece, 128), piece)

    own_copies = [
        pltpu.make_async_copy(
            source_rows.at[:, columns(me, part)],
            gathered.at[part, at(me, ROWS), :],
            local_sem.at[part],
        )
        for part in range(PIECES)
    ]
    own_copies.append(
        pltpu.make_async_copy(own_rotation, rotations.at[at(me, columns_out), :], local_sem.at[PIECES])
    )
    for copy in own_copies:
        copy.start()
    pl.semaphore_wait(barrier, panels - 1)
    rotation_copies = [
        pltpu.make_async_remote_copy(
            src_ref=own_rotation,
            dst_ref=rotations.at[at(me, columns_out), :],
            send_sem=rot_send.at[k],
            recv_sem=rot_recv.at[k],
            device_id={"orb": other},
            device_id_type=MESH,
        )
        for k, other in enumerate(others)
    ]
    panel_copies = [
        [
            pltpu.make_async_remote_copy(
                src_ref=source_rows.at[:, columns(other, part)],
                dst_ref=gathered.at[part, at(me, ROWS), :],
                send_sem=in_send.at[part, k],
                recv_sem=in_recv.at[part, k],
                device_id={"orb": other},
                device_id_type=MESH,
            )
            for k, other in enumerate(others)
        ]
        for part in range(PIECES)
    ]
    for copy in rotation_copies:
        copy.start()
    for part in range(PIECES):
        for copy in panel_copies[part]:
            copy.start()

    own_copies[PIECES].wait()
    for copy in rotation_copies:
        copy.wait()
    span = wide.shape[1]
    every = rotations[...]
    row_of = lax.broadcasted_iota(jnp.int32, (every.shape[1], span), 0)
    for z in range(DEPTH):
        chosen = (row_of == spread_index[...]) & (spread_plane[...] == z)
        product = dot(every, jnp.where(chosen, 1.0, 0.0).astype(HALF)).astype(HALF)
        for d in range(panels):
            wide[pl.ds((d * DEPTH + z) * columns_out, columns_out), :] = product[
                d * columns_out : (d + 1) * columns_out
            ]

    deep = DEPTH * columns_out
    result_copies = []
    back_copies = []
    for part in range(PIECES):
        own_copies[part].wait()
        for copy in panel_copies[part]:
            copy.wait()
        operand = gathered[part]
        half = span // 2
        product = dot(wide[:, :half], operand) + dot(wide[:, half:], operand)
        products[part] = product.astype(HALF)
        copies = [
            pltpu.make_async_remote_copy(
                src_ref=products.at[part, at(other, deep), :],
                dst_ref=landed.at[:, columns(me, part)],
                send_sem=out_send.at[part, k],
                recv_sem=out_recv.at[part, k],
                device_id={"orb": other},
                device_id_type=MESH,
            )
            for k, other in enumerate(others)
        ]
        for copy in copies:
            copy.start()
        landed[:, columns(me, part)] = products[part, at(me, deep), :]
        result_copies.extend(copies)
    for copy in result_copies:
        copy.wait()
    for z in range(DEPTH):
        back = pltpu.make_async_copy(
            landed.at[pl.ds(z * columns_out, columns_out), :],
            rotated.at[:, pl.ds(z * PLANE, PLANE)],
            local_sem.at[z],
        )
        back.start()
        back_copies.append(back)
    for back in back_copies:
        back.wait()


def body(
    slabs,
    panels,
    orbitals,
    potential,
    projector_atom,
    projector_cell,
    projector_value,
    atom_strength,
    ritz_rotation,
    panel_owner,
):
    cell_count = orbitals.shape[1]
    entries = projector_atom.shape[0]
    in_vmem = pl.BlockSpec(memory_space=pltpu.VMEM)
    anywhere = pl.BlockSpec(memory_space=pl.ANY)
    dma = pltpu.SemaphoreType.DMA
    filtered, filtered_rows = pl.pallas_call(
        functools.partial(filter_kernel, slabs),
        out_shape=(
            jax.ShapeDtypeStruct(orbitals.shape, HALF),
            jax.ShapeDtypeStruct((ROWS, PLANE), HALF),
        ),
        in_specs=[in_vmem] * 7 + [anywhere],
        out_specs=(in_vmem, in_vmem),
        scratch_shapes=[
            pltpu.VMEM((PHASES, WINDOW, BLOCK), HALF),
            pltpu.VMEM((2, 3 * ROWS, PLANE), HALF),
            pltpu.VMEM((2, ROWS, PLANE + 2 * PAD), HALF),
            pltpu.VMEM((ROWS, PLANE), FLOAT),
            pltpu.VMEM((ROWS, PLANE), FLOAT),
            pltpu.VMEM((6 * DEPTH * ATOM_SLOTS, entries), HALF),
            pltpu.VMEM((2 * COARSE, entries), HALF),
            pltpu.VMEM((256, PLANE), HALF),
            pltpu.VMEM((2, PANEL, 128), FLOAT),
            pltpu.VMEM((2, 4, PANEL, 128), FLOAT),
            dma,
            dma((2, 2, CHUNKS)),
            dma((2, 2, CHUNKS)),
            dma((2, 4)),
            dma((2, 4)),
        ],
        compiler_params=pltpu.CompilerParams(
            collective_id=0, has_side_effects=True, vmem_limit_bytes=60 * 1024 * 1024
        ),
        name="filter_panel",
    )(
        orbitals,
        potential.reshape(cell_count // 128, 128),
        projector_atom.reshape(1, entries),
        projector_cell.reshape(1, entries),
        projector_value.reshape(1, entries),
        atom_strength.reshape(1, -1),
        jnp.asarray(depth_band()),
        jnp.asarray(plane_bands()),
    )
    step_count, panel_rows, columns_out = ritz_rotation.shape
    chosen = (panel_owner[:, None] == jnp.arange(panels)[None, :]).astype(FLOAT)
    full = jnp.sum(
        ritz_rotation.astype(FLOAT).transpose(2, 0, 1)[:, :, None, :] * chosen[None, :, :, None], axis=1
    ).reshape(columns_out, panels * panel_rows)
    rounded = lax.reduce_precision(full, 8, 7)
    own_rotation = jnp.concatenate([rounded, full - rounded], 1).astype(HALF)
    halves, owners, planes, inner = np.meshgrid(
        np.arange(2), np.arange(panels), np.arange(DEPTH), np.arange(PANEL), indexing="ij"
    )
    spread_index = (halves * panels * PANEL + owners * PANEL + inner).reshape(1, -1).astype(np.int32)
    spread_plane = planes.reshape(1, -1).astype(np.int32)
    span = spread_index.shape[1]
    width = PLANE // panels
    piece = width // PIECES
    rotated = pl.pallas_call(
        functools.partial(rotate_kernel, panels),
        out_shape=jax.ShapeDtypeStruct((columns_out, cell_count), HALF),
        in_specs=[anywhere, in_vmem, in_vmem, in_vmem],
        out_specs=anywhere,
        scratch_shapes=[
            pltpu.VMEM((panels * columns_out, own_rotation.shape[1]), HALF),
            pltpu.VMEM((panels * columns_out * DEPTH, span), HALF),
            pltpu.VMEM((PIECES, panels * ROWS, piece), HALF),
            pltpu.VMEM((PIECES, panels * columns_out * DEPTH, piece), HALF),
            pltpu.VMEM((columns_out * DEPTH, PLANE), HALF),
            dma((DEPTH,)),
            dma((panels - 1,)),
            dma((panels - 1,)),
            dma((PIECES, panels - 1)),
            dma((PIECES, panels - 1)),
            dma((PIECES, panels - 1)),
            dma((PIECES, panels - 1)),
        ],
        compiler_params=pltpu.CompilerParams(
            collective_id=1, has_side_effects=True, vmem_limit_bytes=60 * 1024 * 1024
        ),
        name="rotate_panels",
    )(filtered_rows, own_rotation, jnp.asarray(spread_index), jnp.asarray(spread_plane))
    return (filtered, rotated)


def solution(mesh):
    in_specs = (
        P("orb", "grid"),
        P("grid"),
        P("grid"),
        P("grid"),
        P("grid"),
        P(),
        P(None, None, "orb"),
        P(),
    )
    out_specs = (P("orb", "grid"), P("orb", "grid"))
    local = functools.partial(body, mesh.shape["grid"], mesh.shape["orb"])
    return jax.shard_map(local, mesh=mesh, in_specs=in_specs, out_specs=out_specs, check_vma=False)
```

time: 416 us -> 94.6 us (0.23)
  other arithmetic: 137 us -> 2.21 us
  local copies, waits for them, and re-layouts: 118 us -> 6.94 us
  waiting for transfers between devices: 102 us -> 0 us
  Pallas kernels: 0 us -> 84.4 us
  starting transfers between devices: 29.9 us -> 0 us
  between operations: 22 us -> 0.68 us
  matrix products: 5.62 us -> 0 us
    all_gather x1 -> x0, waiting for transfers between devices: 90.2 us -> none  [from_root(): lax.all_gather(array, axis)]
    pallas_call x0 -> x2, Pallas kernels: none -> 84.4 us  [the longest x1 46.1 us: body(): pl.pallas_call(functools.partial(filter_kernel, slabs), out_shape=(jax.Sh...]
    add x2 -> x0, other arithmetic: 63.8 us -> none  [hamiltonian(): return -0.5 * summed + potential * middle + nonlocal_term]
    scatter-add x2 -> x0, other arithmetic: 52.9 us -> none  [hamiltonian(): nonlocal_term = jnp.zeros_like(middle).at[:, projector_cell].add(spread)]
    scatter-add x2 -> x0, local copies, waits for them, and re-layouts: 30.9 us -> none  [hamiltonian(): nonlocal_term = jnp.zeros_like(middle).at[:, projector_cell].add(spread)]
    add x2 -> x0, local copies, waits for them, and re-layouts: 27.9 us -> none  [hamiltonian(): return -0.5 * summed + potential * middle + nonlocal_term]
    gather x4 -> x0, local copies, waits for them, and re-layouts: 24.4 us -> none  [hamiltonian(): gathered = jnp.take(middle, projector_cell, axis=1)]
    all_to_all x2 -> x0, starting transfers between devices: 16.5 us -> none  [from_everyone(): return lax.all_to_all(copies, axis, split_axis=0, concat_axis=0, tiled=True)]
  transfers between devices with their start and end apart: 7 -> 0, of which waited for: 3 -> 0; matrix products, arithmetic and copies ran while one was open for 17% -> 0% of each run, Pallas kernels for 0% -> 0%
where the time goes in v1:
time: 94.6 us; the launch traced here: 94.2 us
  Pallas kernels  84.4 us (89%)
  local copies, waits for them, and re-layouts  6.94 us (7%)
  other arithmetic  2.21 us (2%)
    pallas_call x1, Pallas kernels, body(): pl.pallas_call(functools.partial(filter_kernel, slabs), out_shape=(jax.Sh...  46.1 us
    pallas_call x1, Pallas kernels, body(): pl.pallas_call(functools.partial(rotate_kernel, panels), out_shape=jax.Sh...  38.3 us
    unnamed x6, local copies, waits for them, and re-layouts  3 us

profile of v1, /device:TPU:1, one launch (start us, length us, event | category | flops | bytes accessed | tf_op | source)
XLA Modules:
  0.0 94.2 jit_solution(13765122156371404152)
XLA Ops:
  0.6 0.7 fusion.1
  1.4 1.3 %reshape.46.atom = s32[1,1536]{1,0:T(1,128)} reshape(s32[1536]{0:T(1024)} %param.14) | data formatting | bytes 12288 | tf_op jit(solution)/shard_map/reshape | solution.py:530
  2.6 1.3 %reshape.47.cell = s32[1,1536]{1,0:T(1,128)} reshape(s32[1536]{0:T(1024)} %param.15) | data formatting | bytes 12288 | tf_op jit(solution)/shard_map/reshape | solution.py:531
  3.9 1.3 %reshape.48.value = f32[1,1536]{1,0:T(1,128)} reshape(f32[1536]{0:T(1024)} %param.16) | data formatting | bytes 12288 | tf_op jit(solution)/shard_map/reshape | solution.py:532
  5.2 0.7 convert_bitcast_fusion
  5.9 0.1 multiply_reduce_fusion
  6.0 0.1 copy.18
  6.1 0.7 pad_maximum_fusion.own_rotation
  6.8 46.1 %filter_panel.1 = (bf16[8,55296]{1,0:T(8,128)(2,1)}, bf16[48,9216]{1,0:T(8,128)(2,1)}) custom-call(bf16[8,55296]{1,0:T(8,128)(2,1)} %orbitals.1, f32[432,128]{1,0:T(8,128)} %bitcast.5, s32[1,1536]{1,0:T(1,128)} %reshape.46.atom, s32[1,1536]{1,0:T(1,128)} %reshape.47.cell, f32[1,1536]{1,0:T(1,128)} %reshape.48.value, f32[1,128]{1,0:T(1,128)} %bitcast.7, ...), custom_call_target="tpu_custom_call" | custom-call | tf_op jit(solution)/shard_map/filter_panel/pallas_call | solution.py:498
  52.9 0.0 copy-start.1
  52.9 38.3 %rotate_panels.1 = bf16[16,55296]{1,0:T(8,128)(2,1)} custom-call(bf16[48,9216]{1,0:T(8,128)(2,1)} %get-tuple-element.5.source_rows, bf16[16,128]{1,0:T(8,128)(2,1)} %pad_maximum_fusion.own_rotation, s32[1,768]{1,0:T(1,128)} %constant.12.clone.spread_index, s32[1,768]{1,0:T(1,128)} %constant.13.clone.spread_plane), custom_call_target="tpu_custom_call" | custom-call | tf_op jit(solution)/shard_map/rotate_panels/pallas_call | solution.py:552
  91.2 0.0 copy-done.1
  91.2 0.0 copy-start
  91.2 0.9 copy.22
  92.1 0.9 copy-done
  93.0 1.2 %copy.23 = bf16[16,55296]{1,0:T(8,128)(2,1)} copy(bf16[16,55296]{1,0:T(8,128)(2,1)S(1)} %copy-done) | data formatting | bytes 3538944
  (1 shorter events, 0.0 us)
Async XLA Ops:
  52.9 38.3 %copy-start.1 = (bf16[8,55296]{1,0:T(8,128)(2,1)S(1)}, bf16[8,55296]{1,0:T(8,128)(2,1)}, u32[]{:S(2)}) copy-start(bf16[8,55296]{1,0:T(8,128)(2,1)} %get-tuple-element.10) | copy-start | bytes 2654212
  91.2 1.8 %copy-start = (bf16[16,55296]{1,0:T(8,128)(2,1)S(1)}, bf16[16,55296]{1,0:T(8,128)(2,1)}, u32[]{:S(2)}) copy-start(bf16[16,55296]{1,0:T(8,128)(2,1)} %rotate_panels.1) | copy-start | bytes 5308420

commit v2 on v1

v2 whole, which is shorter than its diff:
```python
import functools

import jax
import jax.numpy as jnp
import ml_dtypes
import numpy as np
from jax import lax
from jax.experimental import pallas as pl
from jax.experimental.pallas import tpu as pltpu
from jax.sharding import PartitionSpec as P

NX = 96
NY = 96
REACH = 6
ATOM_DEV = 4
PLANE = NX * NY
DEPTH = 6
PANEL = 8
ROWS = DEPTH * PANEL
BLOCK = 256
BLOCKS = PLANE // BLOCK
STRIP = 1024
LANES = 128
PAD = 640
WINDOW = BLOCK + 2 * PAD
PHASES = 3
CHUNKS = 3
CHUNK = PLANE // CHUNKS
CHUNK_STRIPS = CHUNK // STRIP
ATOM_SLOTS = 3 * ATOM_DEV
TABLE = 80
COARSE = 512
GROUPS_PER_TURN = 6
FLOAT = jnp.float32
HALF = jnp.bfloat16
MESH = pl.DeviceIdType.MESH

stencil_weights = (
    -5369.0 / 1800.0,
    12.0 / 7.0,
    -15.0 / 56.0,
    10.0 / 189.0,
    -1.0 / 112.0,
    2.0 / 1925.0,
    -1.0 / 16632.0,
)
cheb_center = 6.0
cheb_half = 6.0
unit = stencil_weights[1]


def plane_bands():
    bands = np.zeros((PHASES, WINDOW, BLOCK), np.float32)
    for phase in range(PHASES):
        target = phase * BLOCK + np.arange(BLOCK)
        source = phase * BLOCK - PAD + np.arange(WINDOW)
        jump = source[:, None] - target[None, :]
        same_row = (source[:, None] // NX) == (target[None, :] // NX)
        for k in range(1, REACH + 1):
            weight = stencil_weights[k] / unit
            bands[phase] += weight * ((np.abs(jump) == k) & same_row)
            bands[phase] += weight * (np.abs(jump) == k * NX)
    return bands.astype(ml_dtypes.bfloat16)


def depth_band():
    band = np.zeros((DEPTH, 3 * DEPTH), np.float32)
    for z in range(DEPTH):
        for k in range(1, REACH + 1):
            band[z, DEPTH + z - k] += stencil_weights[k] / unit
            band[z, DEPTH + z + k] += stencil_weights[k] / unit
    return np.kron(band, np.eye(PANEL, dtype=np.float32))


def contract_last(left, right):
    return lax.dot_general(left, right, (((1,), (1,)), ((), ())), preferred_element_type=FLOAT)


def dot(left, right):
    return jnp.dot(left, right, preferred_element_type=FLOAT)


def fused_kernel(
    slabs,
    panels,
    owners,
    orbitals,
    potential,
    atom,
    cell,
    value,
    strength,
    own_rotation,
    column_facts,
    depth_weights,
    bands_hbm,
    filtered,
    rotated,
    bands,
    stack,
    padded,
    planar,
    step,
    picks,
    spots,
    table,
    found_sums,
    sums_out,
    sums_in,
    rows_out,
    rotations,
    wide,
    gathered,
    products,
    landed,
    band_sem,
    halo_send,
    halo_recv,
    sums_send,
    sums_recv,
    local_sem,
    rot_send,
    rot_recv,
    in_send,
    in_recv,
    out_send,
    out_recv,
):
    me = lax.axis_index("grid")
    seat = lax.axis_index("orb")
    after, before = lax.rem(me + 1, slabs), lax.rem(me + slabs - 1, slabs)
    after2, before2 = lax.rem(me + 2, slabs), lax.rem(me + slabs - 2, slabs)
    others = [lax.rem(seat + k, panels) for k in range(1, panels)]
    barrier = pltpu.get_barrier_semaphore()
    for other in (after, before, after2, before2):
        pl.semaphore_signal(barrier, inc=1, device_id={"grid": other}, device_id_type=MESH)
    for other in others:
        pl.semaphore_signal(barrier, inc=1, device_id={"orb": other}, device_id_type=MESH)
    band_copy = pltpu.make_async_copy(bands_hbm, bands, band_sem)
    band_copy.start()

    def strip(j):
        return pl.ds(pl.multiple_of(j * STRIP, STRIP), STRIP)

    def at(index, size):
        return pl.ds(pl.multiple_of(index * size, size), size)

    def halo_copies(stage, chunk):
        columns = pl.ds(chunk * CHUNK, CHUNK)
        own = stack.at[stage, pl.ds(ROWS, ROWS), columns]
        return [
            pltpu.make_async_remote_copy(
                src_ref=own,
                dst_ref=stack.at[stage, pl.ds(place, ROWS), columns],
                send_sem=halo_send.at[stage, side, chunk],
                recv_sem=halo_recv.at[stage, side, chunk],
                device_id={"grid": other},
                device_id_type=MESH,
            )
            for side, (other, place) in enumerate(((after, 0), (before, 2 * ROWS)))
        ]

    def store_own(stage, j, rows):
        stack[stage, pl.ds(ROWS, ROWS), strip(j)] = rows
        padded[stage, :, pl.ds(pl.multiple_of(PAD + j * STRIP, LANES), STRIP)] = rows

    for chunk in range(CHUNKS):

        def take_block(i, carry, chunk=chunk):
            j = chunk * CHUNK_STRIPS + i
            planes = [
                orbitals[:, pl.ds(pl.multiple_of(z * PLANE + j * STRIP, STRIP), STRIP)].astype(FLOAT)
                for z in range(DEPTH)
            ]
            store_own(0, j, jnp.concatenate(planes, 0).astype(HALF))
            return carry

        lax.fori_loop(0, CHUNK_STRIPS, take_block, 0)
        if chunk == 0:
            pl.semaphore_wait(barrier, 4 + panels - 1)
        for copy in halo_copies(0, chunk):
            copy.start()

    rotation_copies = [
        pltpu.make_async_remote_copy(
            src_ref=own_rotation,
            dst_ref=rotations.at[seat],
            send_sem=rot_send.at[k],
            recv_sem=rot_recv.at[k],
            device_id={"orb": other},
            device_id_type=MESH,
        )
        for k, other in enumerate(others)
    ]
    for copy in rotation_copies:
        copy.start()
    rotations[seat] = own_rotation[...]
    for stage in range(2):
        padded[stage, :, pl.ds(0, PAD)] = jnp.zeros((ROWS, PAD), HALF)
        padded[stage, :, pl.ds(PAD + PLANE, PAD)] = jnp.zeros((ROWS, PAD), HALF)

    def as_row(ref):
        return jnp.concatenate([ref[i : i + 1, :] for i in range(ref.shape[0])], 1)

    cells = as_row(cell)
    plane_of = jnp.zeros_like(cells)
    for z in range(1, DEPTH):
        plane_of = plane_of + (cells >= z * PLANE).astype(jnp.int32)
    in_plane = cells - plane_of * PLANE
    slot = as_row(atom) - (me - 1) * ATOM_DEV
    coarse_key = (in_plane >> 9) * TABLE + plane_of * ATOM_SLOTS + slot
    fine_key = in_plane & (COARSE - 1)
    entries = cells.shape[1]
    values = as_row(value)
    high = values.astype(HALF).astype(FLOAT)
    low = values - high

    def fill_spots(i, carry):
        row = pl.multiple_of(i * 32, 32)
        here = (lax.broadcasted_iota(jnp.int32, (32, entries), 0) + row) == fine_key
        spots[pl.ds(row, 32), :] = jnp.where(here, high, 0.0).astype(HALF)
        spots[pl.ds(row + COARSE, 32), :] = jnp.where(here, low, 0.0).astype(HALF)
        return carry

    lax.fori_loop(0, COARSE // 32, fill_spots, 0)
    groups = PLANE // COARSE
    picked = GROUPS_PER_TURN * TABLE

    def fill_table(turn, carry):
        def fill_picks(i, inner):
            row = pl.multiple_of(i * 32, 32)
            here = (
                lax.broadcasted_iota(jnp.int32, (32, entries), 0) + (row + turn * picked)
            ) == coarse_key
            picks[pl.ds(row, 32), :] = jnp.where(here, 1.0, 0.0).astype(HALF)
            return inner

        lax.fori_loop(0, picked // 32, fill_picks, 0)
        full = contract_last(picks[...], spots[pl.ds(0, COARSE), :]) + contract_last(
            picks[...], spots[pl.ds(COARSE, COARSE), :]
        )
        for i in range(GROUPS_PER_TURN):
            part = full[i * TABLE : (i + 1) * TABLE]
            rounded = part.astype(HALF)
            columns = pl.ds(pl.multiple_of((turn * GROUPS_PER_TURN + i) * COARSE, COARSE), COARSE)
            table[pl.ds(0, TABLE), columns] = rounded
            table[pl.ds(TABLE, TABLE), columns] = (part - rounded.astype(FLOAT)).astype(HALF)
        return carry

    lax.fori_loop(0, groups // GROUPS_PER_TURN, fill_table, 0)

    lanes = lax.broadcasted_iota(jnp.int32, (PANEL, LANES), 1)
    near_strength = pltpu.roll(
        jnp.broadcast_to(strength[...], (PANEL, LANES)),
        lax.rem(LANES + ATOM_DEV - me * ATOM_DEV, LANES),
        1,
    )
    column_of = lax.broadcasted_iota(jnp.int32, (ROWS, 3 * ROWS), 1)
    has_before = (me > 0).astype(FLOAT)
    has_after = (me < slabs - 1).astype(FLOAT)
    keep = jnp.where(
        column_of < ROWS, has_before, jnp.where(column_of >= 2 * ROWS, has_after, 1.0)
    )
    across = (depth_weights[...] * keep).astype(HALF)
    plane_lanes = [(lanes >= z * ATOM_SLOTS) & (lanes < (z + 1) * ATOM_SLOTS) for z in range(DEPTH)]
    partners = ((after, LANES - 4), (before, 4), (after2, LANES - 8), (before2, 8))
    found_sums[...] = jnp.zeros((ROWS, LANES), FLOAT)
    slot_row = lax.broadcasted_iota(jnp.int32, (LANES, 2 * TABLE), 0)
    slot_column = lax.broadcasted_iota(jnp.int32, (LANES, 2 * TABLE), 1)
    to_high = slot_row == slot_column
    to_both = to_high | (slot_row + TABLE == slot_column)
    to_high = jnp.where(to_high & (slot_row < TABLE), 1.0, 0.0).astype(HALF)
    to_both = jnp.where(to_both & (slot_row < TABLE), 1.0, 0.0).astype(HALF)

    def send_sums(stage):
        field = stack[stage, pl.ds(ROWS, ROWS), :]
        found_sums[:, pl.ds(0, TABLE)] = contract_last(
            field, table[pl.ds(0, TABLE), :]
        ) + contract_last(field, table[pl.ds(TABLE, TABLE), :])
        both = found_sums[...]
        own = jnp.zeros((PANEL, LANES), FLOAT)
        for z in range(DEPTH):
            part = jnp.where(plane_lanes[z], both[z * PANEL : (z + 1) * PANEL], 0.0)
            own = own + (part if z == 0 else pltpu.roll(part, LANES - z * ATOM_SLOTS, 1))
        sums_out[stage] = own
        copies = [
            pltpu.make_async_remote_copy(
                src_ref=sums_out.at[stage],
                dst_ref=sums_in.at[stage, k],
                send_sem=sums_send.at[stage, k],
                recv_sem=sums_recv.at[stage, k],
                device_id={"grid": other},
                device_id_type=MESH,
            )
            for k, (other, _) in enumerate(partners)
        ]
        for copy in copies:
            copy.start()
        return copies

    def planar_part(stage):
        for phase in range(PHASES):
            windows = [
                padded[stage, :, pl.ds((i * PHASES + phase) * BLOCK, WINDOW)]
                for i in range(BLOCKS // PHASES)
            ]
            product = dot(jnp.concatenate(windows, 0), bands[phase])
            for i in range(BLOCKS // PHASES):
                planar[:, pl.ds((i * PHASES + phase) * BLOCK, BLOCK)] = product[
                    i * ROWS : (i + 1) * ROWS
                ]

    def coupling(stage, copies):
        for copy in copies:
            copy.wait()
        total = sums_out[stage]
        for k, (_, turn) in enumerate(partners):
            total = total + pltpu.roll(sums_in[stage, k], turn, 1)
        scaled = jnp.where(plane_lanes[0], total * near_strength, 0.0)
        blocks = [
            scaled if z == 0 else pltpu.roll(scaled, z * ATOM_SLOTS, 1) for z in range(DEPTH)
        ]
        spread = jnp.concatenate(blocks, 0)
        rounded = spread.astype(HALF)
        rest = (spread - rounded.astype(FLOAT)).astype(HALF)
        return jnp.concatenate([dot(rounded, to_both), dot(rest, to_high)], 0).astype(HALF)

    def image(stage, j, couplings, middle):
        columns = strip(j)
        neighbours = planar[:, columns] + dot(across, stack[stage, :, columns])
        both = dot(couplings, table[:, columns])
        rows = []
        for z in range(DEPTH):
            pieces = [
                jnp.broadcast_to(
                    potential[pl.ds(z * (PLANE // LANES) + j * (STRIP // LANES) + h, 1), :],
                    (PANEL, LANES),
                )
                for h in range(STRIP // LANES)
            ]
            rows.append(jnp.concatenate(pieces, 1))
        local = (jnp.concatenate(rows, 0) - (1.5 * stencil_weights[0] + cheb_center)) * (
            1.0 / cheb_half
        )
        return (
            middle * local
            - (0.5 * unit / cheb_half) * neighbours
            + (both[:ROWS] + both[ROWS:]) * (1.0 / cheb_half)
        )

    sums = send_sums(0)
    band_copy.wait()
    planar_part(0)
    couplings = coupling(0, sums)
    for chunk in range(CHUNKS):
        for copy in halo_copies(0, chunk):
            copy.wait()

        def first_block(i, carry, chunk=chunk):
            j = chunk * CHUNK_STRIPS + i
            middle = stack[0, pl.ds(ROWS, ROWS), strip(j)].astype(FLOAT)
            field = image(0, j, couplings, middle)
            step[:, strip(j)] = field
            store_own(1, j, field.astype(HALF))
            return carry

        lax.fori_loop(0, CHUNK_STRIPS, first_block, 0)
        for copy in halo_copies(1, chunk):
            copy.start()

    sums = send_sums(1)
    planar_part(1)

    for copy in rotation_copies:
        copy.wait()
    inputs, columns_out = own_rotation.shape
    target = lax.broadcasted_iota(jnp.int32, (panels * columns_out, columns_out), 0)
    member = lax.broadcasted_iota(jnp.int32, (panels * columns_out, columns_out), 1)
    every = jnp.zeros((panels * columns_out, inputs), FLOAT)
    for d in range(panels):
        place = jnp.where(target == member + d * columns_out, 1.0, 0.0).astype(HALF)
        every = every + contract_last(place, rotations[d])
    every = every.astype(HALF)
    span = panels * ROWS
    input_of = lax.broadcasted_iota(jnp.int32, (inputs, span), 0)
    owner_of = jnp.zeros((inputs, span), jnp.int32)
    for s in range(inputs // PANEL):
        inside = (input_of >= s * PANEL) & (input_of < (s + 1) * PANEL)
        owner_of = owner_of + jnp.where(inside, owners[s], 0)
    matches = (owner_of == column_facts[0:1, :]) & (
        (input_of & (PANEL - 1)) == column_facts[2:3, :]
    )
    for z in range(DEPTH):
        chosen = jnp.where(matches & (column_facts[1:2, :] == z), 1.0, 0.0).astype(HALF)
        product = dot(every, chosen)
        rounded = product.astype(HALF)
        rest = (product - rounded.astype(FLOAT)).astype(HALF)
        for d in range(panels):
            place = pl.ds((d * DEPTH + z) * columns_out, columns_out)
            wide[place, pl.ds(0, span)] = rounded[d * columns_out : (d + 1) * columns_out]
            wide[place, pl.ds(span, span)] = rest[d * columns_out : (d + 1) * columns_out]

    piece = CHUNK // panels
    deep = DEPTH * columns_out

    def columns_of(owner, chunk):
        return pl.ds(pl.multiple_of(owner * piece + chunk * CHUNK, LANES), piece)

    def panel_copies(chunk):
        return [
            pltpu.make_async_remote_copy(
                src_ref=rows_out.at[:, columns_of(other, chunk)],
                dst_ref=gathered.at[chunk, at(seat, ROWS), :],
                send_sem=in_send.at[chunk, k],
                recv_sem=in_recv.at[chunk, k],
                device_id={"orb": other},
                device_id_type=MESH,
            )
            for k, other in enumerate(others)
        ]

    couplings = coupling(1, sums)
    for chunk in range(CHUNKS):
        for copy in halo_copies(1, chunk):
            copy.wait()

        def second_block(i, carry, chunk=chunk):
            j = chunk * CHUNK_STRIPS + i
            initial = stack[0, pl.ds(ROWS, ROWS), strip(j)].astype(FLOAT)
            field = 2.0 * image(1, j, couplings, step[:, strip(j)]) - initial
            rows_out[:, strip(j)] = field.astype(HALF)
            return carry

        lax.fori_loop(0, CHUNK_STRIPS, second_block, 0)
        for copy in panel_copies(chunk):
            copy.start()
        gathered[chunk, at(seat, ROWS), :] = rows_out[:, columns_of(seat, chunk)]
    filtered_backs = [
        pltpu.make_async_copy(
            rows_out.at[pl.ds(z * PANEL, PANEL), :],
            filtered.at[:, pl.ds(z * PLANE, PLANE)],
            local_sem.at[0, z],
        )
        for z in range(DEPTH)
    ]
    for copy in filtered_backs:
        copy.start()

    result_copies = []
    for chunk in range(CHUNKS):
        for copy in panel_copies(chunk):
            copy.wait()
        operand = gathered[chunk]
        product = dot(wide[:, pl.ds(0, span)], operand) + dot(wide[:, pl.ds(span, span)], operand)
        products[chunk] = product.astype(HALF)
        copies = [
            pltpu.make_async_remote_copy(
                src_ref=products.at[chunk, at(other, deep), :],
                dst_ref=landed.at[:, columns_of(seat, chunk)],
                send_sem=out_send.at[chunk, k],
                recv_sem=out_recv.at[chunk, k],
                device_id={"orb": other},
                device_id_type=MESH,
            )
            for k, other in enumerate(others)
        ]
        for copy in copies:
            copy.start()
        landed[:, columns_of(seat, chunk)] = products[chunk, at(seat, deep), :]
        result_copies.extend(copies)
    for copy in filtered_backs:
        copy.wait()
    for copy in result_copies:
        copy.wait()
    rotated_backs = [
        pltpu.make_async_copy(
            landed.at[pl.ds(z * columns_out, columns_out), :],
            rotated.at[:, pl.ds(z * PLANE, PLANE)],
            local_sem.at[1, z],
        )
        for z in range(DEPTH)
    ]
    for copy in rotated_backs:
        copy.start()
    for copy in rotated_backs:
        copy.wait()


def body(
    slabs,
    panels,
    orbitals,
    potential,
    projector_atom,
    projector_cell,
    projector_value,
    atom_strength,
    ritz_rotation,
    panel_owner,
):
    cell_count = orbitals.shape[1]
    entries = projector_atom.shape[0]
    steps, panel_rows, columns_out = ritz_rotation.shape
    in_vmem = pl.BlockSpec(memory_space=pltpu.VMEM)
    anywhere = pl.BlockSpec(memory_space=pl.ANY)
    dma = pltpu.SemaphoreType.DMA
    owner, plane, inner = np.meshgrid(
        np.arange(panels), np.arange(DEPTH), np.arange(PANEL), indexing="ij"
    )
    column_facts = np.zeros((8, panels * ROWS), np.int32)
    column_facts[:3] = [owner.ravel(), plane.ravel(), inner.ravel()]
    piece = CHUNK // panels
    deep = DEPTH * columns_out
    return pl.pallas_call(
        functools.partial(fused_kernel, slabs, panels),
        out_shape=(
            jax.ShapeDtypeStruct(orbitals.shape, HALF),
            jax.ShapeDtypeStruct((columns_out, cell_count), HALF),
        ),
        in_specs=[pl.BlockSpec(memory_space=pltpu.SMEM)] + [in_vmem] * 9 + [anywhere],
        out_specs=(anywhere, anywhere),
        scratch_shapes=[
            pltpu.VMEM((PHASES, WINDOW, BLOCK), HALF),
            pltpu.VMEM((2, 3 * ROWS, PLANE), HALF),
            pltpu.VMEM((2, ROWS, PLANE + 2 * PAD), HALF),
            pltpu.VMEM((ROWS, PLANE), FLOAT),
            pltpu.VMEM((ROWS, PLANE), FLOAT),
            pltpu.VMEM((GROUPS_PER_TURN * TABLE, entries), HALF),
            pltpu.VMEM((2 * COARSE, entries), HALF),
            pltpu.VMEM((2 * TABLE, PLANE), HALF),
            pltpu.VMEM((ROWS, LANES), FLOAT),
            pltpu.VMEM((2, PANEL, LANES), FLOAT),
            pltpu.VMEM((2, 4, PANEL, LANES), FLOAT),
            pltpu.VMEM((ROWS, PLANE), HALF),
            pltpu.VMEM((panels, steps * panel_rows, columns_out), HALF),
            pltpu.VMEM((panels * deep, 2 * panels * ROWS), HALF),
            pltpu.VMEM((CHUNKS, panels * ROWS, piece), HALF),
            pltpu.VMEM((CHUNKS, panels * deep, piece), HALF),
            pltpu.VMEM((deep, PLANE), HALF),
            dma,
            dma((2, 2, CHUNKS)),
            dma((2, 2, CHUNKS)),
            dma((2, 4)),
            dma((2, 4)),
            dma((2, DEPTH)),
            dma((panels - 1,)),
            dma((panels - 1,)),
            dma((CHUNKS, panels - 1)),
            dma((CHUNKS, panels - 1)),
            dma((CHUNKS, panels - 1)),
            dma((CHUNKS, panels - 1)),
        ],
        compiler_params=pltpu.CompilerParams(
            collective_id=0, has_side_effects=True, vmem_limit_bytes=60 * 1024 * 1024
        ),
        name="fused_filter",
    )(
        panel_owner,
        orbitals,
        potential.reshape(cell_count // LANES, LANES),
        projector_atom.reshape(entries // LANES, LANES),
        projector_cell.reshape(entries // LANES, LANES),
        projector_value.reshape(entries // LANES, LANES),
        atom_strength.reshape(1, -1),
        ritz_rotation.reshape(steps * panel_rows, columns_out),
        jnp.asarray(column_facts),
        jnp.asarray(depth_band()),
        jnp.asarray(plane_bands()),
    )


def solution(mesh):
    in_specs = (
        P("orb", "grid"),
        P("grid"),
        P("grid"),
        P("grid"),
        P("grid"),
        P(),
        P(None, None, "orb"),
        P(),
    )
    out_specs = (P("orb", "grid"), P("orb", "grid"))
    local = functools.partial(body, mesh.shape["grid"], mesh.shape["orb"])
    return jax.shard_map(local, mesh=mesh, in_specs=in_specs, out_specs=out_specs, check_vma=False)
```

time: 94.6 us -> 76.6 us (0.81)
  Pallas kernels: 84.4 us -> 72.2 us
  local copies, waits for them, and re-layouts: 6.94 us -> 3.48 us
  other arithmetic: 2.21 us -> 0 us
    pallas_call x2 -> x1, Pallas kernels: 84.4 us -> 72.2 us  [body(): pl.pallas_call(functools.partial(fused_kernel, slabs, panels), out_shape=...]
    reshape x4 -> x0, local copies, waits for them, and re-layouts: 3.94 us -> none  [the longest x1 1.29 us: body(): projector_atom.reshape(1, entries)]
    unnamed x6 -> x4, local copies, waits for them, and re-layouts: 3 us -> 3.48 us
where the time goes in v2:
time: 76.6 us; the launch traced here: 76.3 us
  Pallas kernels  72.2 us (94%)
  local copies, waits for them, and re-layouts  3.48 us (5%)
    pallas_call x1, Pallas kernels, body(): pl.pallas_call(functools.partial(fused_kernel, slabs, panels), out_shape=...  72.2 us
    unnamed x4, local copies, waits for them, and re-layouts  3.48 us

profile of v2, /device:TPU:1, one launch (start us, length us, event | category | flops | bytes accessed | tf_op | source)
XLA Modules:
  0.0 76.3 jit_solution(17846744089430932628)
XLA Ops:
  0.6 72.2 %fused_filter.1 = (bf16[8,55296]{1,0:T(8,128)(2,1)}, bf16[16,55296]{1,0:T(8,128)(2,1)}) custom-call(s32[4]{0:T(128)} %owners.1, bf16[8,55296]{1,0:T(8,128)(2,1)} %orbitals.1, f32[432,128]{1,0:T(8,128)} %bitcast.6, s32[12,128]{1,0:T(8,128)} %bitcast.7, s32[12,128]{1,0:T(8,128)} %bitcast.8, f32[12,128]{1,0:T(8,128)} %bitcast.9, f32[1,128]{1,0:T(1,128)} %bitcast.11, ...), custom_call_target="tpu_custom_call" | custom-call | tf_op jit(solution)/shard_map/fused_filter/pallas_call | solution.py:514
  72.9 0.0 copy-start
  72.9 2.3 %copy.15 = bf16[8,55296]{1,0:T(8,128)(2,1)} copy(bf16[8,55296]{1,0:T(8,128)(2,1)} %get-tuple-element.4) | data formatting | bytes 1769472
  75.1 0.0 copy-done
  75.1 1.2 %copy.16 = bf16[16,55296]{1,0:T(8,128)(2,1)} copy(bf16[16,55296]{1,0:T(8,128)(2,1)S(1)} %copy-done) | data formatting | bytes 3538944
Async XLA Ops:
  72.9 2.3 %copy-start = (bf16[16,55296]{1,0:T(8,128)(2,1)S(1)}, bf16[16,55296]{1,0:T(8,128)(2,1)}, u32[]{:S(2)}) copy-start(bf16[16,55296]{1,0:T(8,128)(2,1)} %get-tuple-element.5) | copy-start | bytes 5308420
